TPU v7x, 32 devices: a whole 2x2x4 slice. The times are simulated.
32 devices in a mesh: param: 4 (over y, x), ex: 8 (over z, core).
Axes of the slice: x: 2, y: 2, z: 4, core: 2. Of those that a mesh axis runs over, the one named last changes fastest.
Arguments:
- activations: bfloat16 [64, 32, 4096], P('ex', None, 'param'), may hold values from -24 to 24
- output_gradients: bfloat16 [2, 64, 32, 4096], P(None, 'ex', None, 'param'), may hold values from -24 to 24
- down_projection_weight: bfloat16 [2, 16, 4096], P(None, None, 'param'), may hold values from -0.09375 to 0.09375
- adapter_up: bfloat16 [2, 4096, 16], P(None, 'param'), may hold values from -0.09375 to 0.09375
- projection: bfloat16 [262144, 4096], P(('param', 'ex')), may hold values from -0.111328125 to 0.111328125
- domains: int32 [64], P('ex'), may hold values from 0 to 3
- target_ids: int32 [256], P('param'), may hold values from 0 to 63
Outputs:
- scores: float32 [256, 64], P('param', 'ex')
- domain_scores: float32 [256, 4], P('param')
All inputs are finite; a program needn't handle non-finite values.
Results may differ from a plain program's by a relative error of at most 0.0059.
Values may be sent and summed in bfloat16 or wider, within the bound.
No kernel may reach another device: no remote copies, remote signals or barrier semaphores. Data moves between devices by JAX's collectives and lax.ppermute only.
A program may use at most 192 MiB of HBM per device.

v0:
```python
import math
import jax
import jax.numpy as jnp
from jax import lax
from jax.sharding import PartitionSpec as P

K = 4096
DOMAINS = 4


def inner_rows(left, right):
    return lax.dot_general(
        left,
        right,
        (((0,), (0,)), ((), ())),
        precision=lax.Precision.HIGHEST,
        preferred_element_type=jnp.float32,
    )


def local(
    activations,
    output_gradients,
    down_projection_weight,
    adapter_up,
    projection,
    domains,
    target_ids,
):
    single_float = jnp.float32
    ex_rows = activations.shape[0]
    adapter_rank_size = down_projection_weight.shape[1]
    up_terms = jnp.einsum(
        "ansd,adr->ansr", output_gradients, adapter_up, preferred_element_type=single_float
    )
    down_terms = jnp.einsum(
        "nsd,ard->ansr", activations, down_projection_weight, preferred_element_type=single_float
    )
    partial_low = jnp.concatenate([up_terms[0], up_terms[1], down_terms[0], down_terms[1]], axis=-1)
    rank_factor = lax.psum(partial_low, "param").astype(jnp.bfloat16)
    first = jnp.einsum(
        "erb,ery->eby",
        activations,
        rank_factor[..., : 2 * adapter_rank_size],
        preferred_element_type=single_float,
    )
    second = jnp.einsum(
        "fai,fav->fiv",
        output_gradients[0],
        rank_factor[..., 2 * adapter_rank_size : 3 * adapter_rank_size],
        preferred_element_type=single_float,
    )
    third = jnp.einsum(
        "fai,fav->fiv",
        output_gradients[1],
        rank_factor[..., 3 * adapter_rank_size :],
        preferred_element_type=single_float,
    )
    grads = jnp.concatenate([first, second, third], axis=-1).astype(jnp.bfloat16)
    grads = grads.reshape(ex_rows, grads.shape[1] * grads.shape[2])
    column_indices = lax.all_to_all(grads, "ex", split_axis=1, concat_axis=0, tiled=True)
    features = lax.psum_scatter(
        lax.dot_general(
            projection,
            column_indices,
            (((0,), (1,)), ((), ())),
            preferred_element_type=single_float,
        ),
        ("param", "ex"),
        scatter_dimension=0,
        tiled=True,
    )
    totals = lax.psum(jnp.sum(features * features, axis=0), ("param", "ex"))
    unit_rows = features * lax.rsqrt(totals + 1e-06)[None, :]
    gram = lax.psum(inner_rows(unit_rows, unit_rows), ("param", "ex"))
    example_count = gram.shape[0]
    kernel = gram + 0.25 * jnp.eye(example_count, dtype=single_float)
    lower = jnp.linalg.cholesky(kernel)
    first_row = lax.axis_index("ex") * ex_rows
    picks = (
        jnp.arange(example_count, dtype=jnp.int32)[:, None]
        == first_row + jnp.arange(ex_rows, dtype=jnp.int32)[None, :]
    ).astype(single_float)
    inverse_cols = jax.scipy.linalg.cho_solve((lower, True), picks)
    cross = jnp.take(gram, target_ids, axis=0)
    selfmask = target_ids[:, None] == jnp.arange(example_count, dtype=jnp.int32)[None, :]
    cross = jnp.where(selfmask, jnp.zeros_like(cross), cross)
    scores = math.sqrt(K) * jnp.dot(
        cross, inverse_cols, precision=lax.Precision.HIGHEST, preferred_element_type=single_float
    )
    indicator_matrix = (domains[:, None] == jnp.arange(DOMAINS, dtype=jnp.int32)[None, :]).astype(
        single_float
    )
    domain_partial_sums = jnp.dot(
        scores,
        indicator_matrix,
        precision=lax.Precision.HIGHEST,
        preferred_element_type=single_float,
    )
    domain_scores = lax.psum(domain_partial_sums, "ex") / math.sqrt(example_count / DOMAINS)
    return (scores, domain_scores)


def solution(mesh):
    in_specs = (
        P("ex", None, "param"),
        P(None, "ex", None, "param"),
        P(None, None, "param"),
        P(None, "param", None),
        P(("param", "ex"), None),
        P("ex"),
        P("param"),
    )
    out_specs = (P("param", "ex"), P("param", None))
    return jax.shard_map(local, mesh=mesh, in_specs=in_specs, out_specs=out_specs, check_vma=False)
```

profile of v0, /device:TPU:0, one launch (start us, length us, event | category | flops | bytes accessed | tf_op | source)
XLA Modules:
  0.0 345.9 jit_solution(10288716785213548179)
XLA Ops:
  7.2 0.0 reduce-scatter.2.cloned.1.call-start
  7.2 1.0 copy-done
  8.2 1.3 convolution_bitcast_fusion.1
  9.6 2.0 fusion.11
  11.7 22.6 %psum.28 = bf16[8,32,64]{1,2,0:T(8,128)(2,1)S(1)} all-reduce(f32[8,32,64]{1,2,0:T(8,128)S(1)} %pad_maximum_fusion.1), channel_id=1, replica_groups=mesh['param'=4,'ex'=8] {'param'}, use_global_device_ids=true, to_apply=%region_0.0 | all-reduce | flops 16384 | bytes 98304 | tf_op jit(solution)/shard_map/psum | solution.py:40
  34.3 0.3 fusion
  34.6 0.2 fusion.1
  34.8 0.2 fusion.2
  35.0 1.1 pad_maximum_fusion
  36.1 2.0 copy.13
  38.2 2.5 convert_element_type.13
  40.7 1.8 copy.14
  42.5 31.3 %all_to_all.16 = bf16[8,8,8192]{2,0,1:T(8,128)(2,1)S(1)} all-to-all(bf16[8,8,8192]{2,0,1:T(8,128)(2,1)S(1)} %copy.14), channel_id=1, replica_groups=mesh['param'=4,'ex'=8] {'ex'}, dimensions={1} | all-to-all | bytes 2097152 | tf_op jit(solution)/shard_map/all_to_all | solution.py:61
  73.7 24.4 %convolution_bitcast_fusion = f32[4096,64]{0,1:T(8,128)} fusion(bf16[8192,4096]{1,0:T(8,128)(2,1)} %param.11, bf16[8,8,8192]{2,0,1:T(8,128)(2,1)S(1)} %all_to_all.16), kind=kOutput, calls=%fused_computation.1 | convolution fusion | flops 4294967296 | bytes 69206016 | tf_op jit(solution)/shard_map/dot_general | solution.py:63
  98.1 0.0 reduce-scatter.2.cloned.1.call-update
  98.2 132.3 %reduce-scatter.2.cloned.1.call-done = f32[128,64]{0,1:T(8,128)} async-done(((f32[4096,64]{0,1:T(8,128)}), f32[128,64]{0,1:T(8,128)}) %reduce-scatter.2.cloned.1.call-update) | async-done | bytes 32784 | tf_op jit(solution)/shard_map/reduce_scatter | solution.py:62
  230.5 0.9 multiply_reduce_fusion
  231.3 36.9 %psum.29 = f32[64]{0:T(128)S(1)} all-reduce(f32[64]{0:T(128)S(1)} %multiply_reduce_fusion), channel_id=1, replica_groups=mesh['param'=4,'ex'=8] {'param','ex'}, use_global_device_ids=true, to_apply=%region_3.0 | all-reduce | flops 64 | bytes 512 | tf_op jit(solution)/shard_map/psum | solution.py:73
  268.2 1.1 fusion.23
  269.3 41.6 %psum.30 = f32[64,64]{1,0:T(8,128)S(1)} all-reduce(f32[64,64]{1,0:T(8,128)S(1)} %fusion.23), channel_id=1, replica_groups=mesh['param'=4,'ex'=8] {'param','ex'}, use_global_device_ids=true, to_apply=%region_4.0 | all-reduce | flops 4096 | bytes 32768 | tf_op jit(solution)/shard_map/psum | solution.py:75
  310.9 0.1 copy.15
  311.0 5.8 %cholesky.15 = f32[64,64]{1,0:T(8,128)S(1)} custom-call(f32[64,64]{1,0:T(8,128)S(1)} %fusion.20), custom_call_target="Cholesky" | custom-call | tf_op jit(solution)/shard_map/jit(cholesky)/cholesky | solution.py:78
  316.9 0.6 compare_reduce_fusion
  317.5 0.7 fusion.13
  318.2 4.9 %custom-call.10 = f32[1,64,64]{1,2,0:T(8,128)S(1)} custom-call(f32[1,64,64]{2,1,0:T(8,128)S(1)} %fusion.13), custom_call_target="InvertDiagBlocksLowerTriangular" | custom-call | tf_op jit(solution)/shard_map/jit(_cho_solve)/triangular_solve | solution.py:84
  323.1 0.2 fusion.18
  323.3 0.2 fusion.16
  323.5 0.6 gather_fusion
  324.1 0.2 convolution_multiply_fusion
  324.3 0.3 fusion.31
  324.6 13.9 %psum.31 = f32[64,4]{0,1:T(4,128)S(1)} all-reduce(f32[64,4]{0,1:T(4,128)S(1)} %fusion.31), channel_id=1, replica_groups=mesh['param'=4,'ex'=8] {'ex'}, use_global_device_ids=true, to_apply=%region_7.8 | all-reduce | flops 256 | bytes 2048 | tf_op jit(solution)/shard_map/psum | solution.py:100
  338.4 0.6 broadcast_multiply_fusion
  (19 shorter events, 0.2 us)
Async XLA Ops:
  7.2 1.0 copy-start
  7.2 27.4 %copy-start.1 = (bf16[2,8,32,1024]{3,2,1,0:T(8,128)(2,1)S(1)}, bf16[2,8,32,1024]{3,2,1,0:T(8,128)(2,1)}, u32[]{:S(2)}) copy-start(bf16[2,8,32,1024]{3,2,1,0:T(8,128)(2,1)} %param.8) | copy-start | bytes 3145732
  7.2 223.3 %reduce-scatter.2.cloned.1.call-start = ((), (), s32[]{:S(2)}) async-start(), calls=%async_computation.2 | async-start | bytes 1081344 | tf_op jit(solution)/shard_map/reduce_scatter | solution.py:62
  73.7 24.4 %copy-start.2 = (s32[64]{0:T(128)S(1)}, s32[64]{0:T(128)}, u32[]{:S(2)}) copy-start(s32[64]{0:T(128)} %param.13) | copy-start | bytes 772
  73.7 250.6 %copy-start.3 = (s32[8]{0:T(128)S(1)}, s32[8]{0:T(128)}, u32[]{:S(2)}) copy-start(s32[8]{0:T(128)} %param.12) | copy-start | bytes 100
  324.3 14.7 %copy-start.4 = (f32[64,8]{0,1:T(8,128)}, f32[64,8]{0,1:T(8,128)S(1)}, u32[]{:S(2)}) copy-start(f32[64,8]{0,1:T(8,128)S(1)} %convolution_multiply_fusion) | copy-start | bytes 6148
Sparse Core Ops, SparseCore 0:
  98.3 132.1 reduce-scatter.1
where the time goes:
time: 346 us
  blocking collectives  146 us (42%)
  waiting for transfers between devices  132 us (38%)
  matrix products  30.4 us (9%)
  other arithmetic  14.7 us (4%)
  between operations  14.2 us (4%)
  local copies, waits for them, and re-layouts  8.06 us (2%)
    reduce_scatter x1, waiting for transfers between devices, local(): lax.psum_scatter(lax.dot_general(projection, column_indices, (((0,), (1,)...  132 us
    psum x1, blocking collectives, local(): gram = lax.psum(inner_rows(unit_rows, unit_rows), ('param', 'ex'))  41.6 us
    psum x1, blocking collectives, local(): totals = lax.psum(jnp.sum(features * features, axis=0), ('param', 'ex'))  36.9 us
    all_to_all x1, blocking collectives, local(): lax.all_to_all(grads, 'ex', split_axis=1, concat_axis=0, tiled=True)  31.3 us
    dot_general x1, matrix products, local(): lax.dot_general(projection, column_indices, (((0,), (1,)), ((), ())), pre...  24.4 us
    psum x1, blocking collectives, local(): rank_factor = lax.psum(partial_low, 'param').astype(jnp.bfloat16)  22.6 us
    psum x1, blocking collectives, local(): lax.psum(domain_partial_sums, 'ex') / math.sqrt(example_count / DOMAINS)  13.9 us
  transfers between devices with their start and end apart: 1, of which 1 were waited for; matrix products, arithmetic and copies ran while one was open for 0% of the time, Pallas kernels for 0%

commit v1 on v0

--- a/solution.py
+++ b/solution.py
@@ -6,6 +6,17 @@
 
 K = 4096
 DOMAINS = 4
+
+
+def in_blocks(array, dim, count):
+    before, after = (array.shape[:dim], array.shape[dim + 1 :])
+    return jnp.moveaxis(array.reshape(*before, count, -1, *after), dim, 0)
+
+
+def joined_along(parts, dim):
+    shape = list(parts.shape[1:])
+    shape[dim] *= parts.shape[0]
+    return jnp.moveaxis(parts, 0, dim).reshape(shape)
 
 
 def inner_rows(left, right):
@@ -58,7 +69,15 @@
     )
     grads = jnp.concatenate([first, second, third], axis=-1).astype(jnp.bfloat16)
     grads = grads.reshape(ex_rows, grads.shape[1] * grads.shape[2])
-    column_indices = lax.all_to_all(grads, "ex", split_axis=1, concat_axis=0, tiled=True)
+    size, place = (lax.axis_size("ex"), lax.axis_index("ex"))
+    blocks = in_blocks(grads, 1, size)
+    filled = blocks
+    for hop in range(1, size):
+        target, source = ((place + hop) % size, (place - hop) % size)
+        sent = lax.dynamic_index_in_dim(blocks, target, 0)
+        other = lax.ppermute(sent, "ex", [(i, (i + hop) % size) for i in range(size)])
+        filled = lax.dynamic_update_slice_in_dim(filled, other, source, axis=0)
+    column_indices = joined_along(filled, 0)
     features = lax.psum_scatter(
         lax.dot_general(
             projection,

time: 346 us -> 381 us (1.10)
  blocking collectives: 146 us -> 115 us
  local copies, waits for them, and re-layouts: 8.06 us -> 37.1 us
  waiting for transfers between devices: 132 us -> 156 us
  starting transfers between devices: 0.04 us -> 13.2 us
    all_to_all x1 -> x0, blocking collectives: 31.3 us -> none  [local(): lax.all_to_all(grads, 'ex', split_axis=1, concat_axis=0, tiled=True)]
    dynamic_update_slice x0 -> x7, local copies, waits for them, and re-layouts: none -> 27.5 us  [local(): filled = lax.dynamic_update_slice_in_dim(filled, other, source, axis=0)]
    ppermute x0 -> x7, starting transfers between devices: none -> 13.2 us  [local(): lax.ppermute(sent, 'ex', [(i, (i + hop) % size) for i in range(size)])]
    reduce_scatter x1, waiting for transfers between devices: 132 us -> 145 us  [local(): lax.psum_scatter(lax.dot_general(projection, column_indices, (((0,), (1,)...]
    ppermute x0 -> x7, waiting for transfers between devices: none -> 11.8 us  [local(): lax.ppermute(sent, 'ex', [(i, (i + hop) % size) for i in range(size)])]
  transfers between devices with their start and end apart: 1 -> 8, of which waited for: 1 -> 3; matrix products, arithmetic and copies ran while one was open for 0% -> 6% of each run, Pallas kernels for 0% -> 0%
where the time goes in v1:
time: 381 us; the launch traced here: 380 us
  waiting for transfers between devices  156 us (41%)
  blocking collectives  115 us (30%)
  local copies, waits for them, and re-layouts  37.1 us (10%)
  matrix products  30.4 us (8%)
  between operations  14.5 us (4%)
  other arithmetic  13.7 us (4%)
  starting transfers between devices  13.2 us (3%)
    reduce_scatter x1, waiting for transfers between devices, local(): lax.psum_scatter(lax.dot_general(projection, column_indices, (((0,), (1,)...  145 us
    psum x1, blocking collectives, local(): gram = lax.psum(inner_rows(unit_rows, unit_rows), ('param', 'ex'))  41.8 us
    psum x1, blocking collectives, local(): totals = lax.psum(jnp.sum(features * features, axis=0), ('param', 'ex'))  36.9 us
    dynamic_update_slice x7, local copies, waits for them, and re-layouts, local(): filled = lax.dynamic_update_slice_in_dim(filled, other, source, axis=0)  27.5 us
    dot_general x1, matrix products, local(): lax.dot_general(projection, column_indices, (((0,), (1,)), ((), ())), pre...  24.3 us
    psum x1, blocking collectives, local(): rank_factor = lax.psum(partial_low, 'param').astype(jnp.bfloat16)  22.6 us
    psum x1, blocking collectives, local(): lax.psum(domain_partial_sums, 'ex') / math.sqrt(example_count / DOMAINS)  13.8 us
    ppermute x7, starting transfers between devices, local(): lax.ppermute(sent, 'ex', [(i, (i + hop) % size) for i in range(size)])  13.2 us
  transfers between devices with their start and end apart: 8, of which 3 were waited for; matrix products, arithmetic and copies ran while one was open for 6% of the time, Pallas kernels for 0%

profile of v1, /device:TPU:0, one launch (start us, length us, event | category | flops | bytes accessed | tf_op | source)
XLA Modules:
  0.0 380.4 jit_solution(6355711898327513600)
XLA Ops:
  7.3 0.9 copy-done
  8.2 1.4 convolution_bitcast_fusion.1
  9.6 2.0 fusion.12
  11.7 22.6 %psum.28 = bf16[8,32,64]{1,2,0:T(8,128)(2,1)S(1)} all-reduce(f32[8,32,64]{1,2,0:T(8,128)S(1)} %pad_maximum_fusion.1), channel_id=1, replica_groups=mesh['param'=4,'ex'=8] {'param'}, use_global_device_ids=true, to_apply=%region_0.0 | all-reduce | flops 16384 | bytes 98304 | tf_op jit(solution)/shard_map/psum | solution.py:51
  35.2 1.8 copy.10
  37.0 3.3 convert_element_type.12
  40.4 2.9 dynamic-slice_bitcast_fusion
  43.2 1.6 collective-permute-start.1
  44.8 2.6 collective-permute-start.2
  47.4 1.2 collective-permute-start.3
  48.6 1.2 collective-permute-start.4
  49.8 3.5 collective-permute-done
  53.3 1.6 collective-permute-start.5
  54.9 5.0 %collective-permute-start.6 = (bf16[1,8,8192]{2,0,1:T(2,128)(2,1)}, bf16[1,8,8192]{2,0,1:T(2,128)(2,1)S(1)}, u32[]{:S(2)}, u32[]{:S(2)}) collective-permute-start(bf16[1,8,8192]{2,0,1:T(2,128)(2,1)} %get-tuple-element.2), channel_id=1, source_target_pairs={{0,7},{1,0},{2,1},{3,2},{4,3},{5,4},{6,5},{7,6},{8,15},{9,8},{10,9... | collective-permute-start | bytes 393224 | tf_op jit(solution)/shard_map/ppermute | solution.py:78
  59.9 3.9 %dynamic_update_slice.21 = bf16[8,8,8192]{2,0,1:T(8,128)(2,1)S(1)} dynamic-update-slice(bf16[8,8,8192]{2,0,1:T(8,128)(2,1)S(1)} %bitcast.72, bf16[1,8,8192]{2,0,1:T(2,128)(2,1)S(1)} %collective-permute-done, s32[]{:T(128)S(6)} %select_n.123, s32[]{:T(128)} %constant.162.clone.1, s32[]{:T(128)} %constant.162.clone.1) | dynamic-update-slice | bytes 262148 | tf_op jit(solution)/shard_map/dynamic_update_slice | solution.py:79
  63.8 3.9 %dynamic_update_slice.22 = bf16[8,8,8192]{2,0,1:T(8,128)(2,1)S(1)} dynamic-update-slice(bf16[8,8,8192]{2,0,1:T(8,128)(2,1)S(1)} %dynamic_update_slice.21, bf16[1,8,8192]{2,0,1:T(2,128)(2,1)S(1)} %collective-permute-done.1, s32[]{:T(128)S(6)} %select_n.127, s32[]{:T(128)} %constant.162.clone.1, s32[]{:T(128)} %constant.162.clone.1) | dynamic-update-slice | bytes 262148 | tf_op jit(solution)/shard_map/dynamic_update_slice | solution.py:79
  67.8 8.3 %collective-permute-done.2 = bf16[1,8,8192]{2,0,1:T(2,128)(2,1)S(1)} collective-permute-done((bf16[1,8,8192]{2,0,1:T(2,128)(2,1)}, bf16[1,8,8192]{2,0,1:T(2,128)(2,1)S(1)}, u32[]{:S(2)}, u32[]{:S(2)}) %collective-permute-start.2) | collective-permute-done | bytes 131104 | tf_op jit(solution)/shard_map/ppermute | solution.py:78
  76.1 3.9 %dynamic_update_slice.23 = bf16[8,8,8192]{2,0,1:T(8,128)(2,1)S(1)} dynamic-update-slice(bf16[8,8,8192]{2,0,1:T(8,128)(2,1)S(1)} %dynamic_update_slice.22, bf16[1,8,8192]{2,0,1:T(2,128)(2,1)S(1)} %collective-permute-done.2, s32[]{:T(128)S(6)} %select_n.131, s32[]{:T(128)} %constant.162.clone.1, s32[]{:T(128)} %constant.162.clone.1) | dynamic-update-slice | bytes 262148 | tf_op jit(solution)/shard_map/dynamic_update_slice | solution.py:79
  80.0 3.9 %dynamic_update_slice.24 = bf16[8,8,8192]{2,0,1:T(8,128)(2,1)S(1)} dynamic-update-slice(bf16[8,8,8192]{2,0,1:T(8,128)(2,1)S(1)} %dynamic_update_slice.23, bf16[1,8,8192]{2,0,1:T(2,128)(2,1)S(1)} %collective-permute-done.3, s32[]{:T(128)S(6)} %select_n.135, s32[]{:T(128)} %constant.162.clone.1, s32[]{:T(128)} %constant.162.clone.1) | dynamic-update-slice | bytes 262148 | tf_op jit(solution)/shard_map/dynamic_update_slice | solution.py:79
  83.9 3.9 %dynamic_update_slice.25 = bf16[8,8,8192]{2,0,1:T(8,128)(2,1)S(1)} dynamic-update-slice(bf16[8,8,8192]{2,0,1:T(8,128)(2,1)S(1)} %dynamic_update_slice.24, bf16[1,8,8192]{2,0,1:T(2,128)(2,1)S(1)} %collective-permute-done.4, s32[]{:T(128)S(6)} %select_n.139, s32[]{:T(128)} %constant.162.clone.1, s32[]{:T(128)} %constant.162.clone.1) | dynamic-update-slice | bytes 262148 | tf_op jit(solution)/shard_map/dynamic_update_slice | solution.py:79
  87.9 3.9 %dynamic_update_slice.26 = bf16[8,8,8192]{2,0,1:T(8,128)(2,1)S(1)} dynamic-update-slice(bf16[8,8,8192]{2,0,1:T(8,128)(2,1)S(1)} %dynamic_update_slice.25, bf16[1,8,8192]{2,0,1:T(2,128)(2,1)S(1)} %collective-permute-done.5, s32[]{:T(128)S(6)} %select_n.143, s32[]{:T(128)} %constant.162.clone.1, s32[]{:T(128)} %constant.162.clone.1) | dynamic-update-slice | bytes 262148 | tf_op jit(solution)/shard_map/dynamic_update_slice | solution.py:79
  91.8 3.9 %dynamic_update_slice.27 = bf16[8,8,8192]{2,0,1:T(8,128)(2,1)S(1)} dynamic-update-slice(bf16[8,8,8192]{2,0,1:T(8,128)(2,1)S(1)} %dynamic_update_slice.26, bf16[1,8,8192]{2,0,1:T(2,128)(2,1)S(1)} %collective-permute-done.6, s32[]{:T(128)S(6)} %select_n.147, s32[]{:T(128)} %constant.162.clone.1, s32[]{:T(128)} %constant.162.clone.1) | dynamic-update-slice | bytes 262148 | tf_op jit(solution)/shard_map/dynamic_update_slice | solution.py:79
  95.8 24.3 %convolution_bitcast_fusion = f32[4096,64]{0,1:T(8,128)} fusion(bf16[8192,4096]{1,0:T(8,128)(2,1)} %param.11, bf16[8,8,8192]{2,0,1:T(8,128)(2,1)S(1)} %dynamic_update_slice.27), kind=kOutput, calls=%fused_computation.1 | convolution fusion | flops 4294967296 | bytes 69206016 | tf_op jit(solution)/shard_map/dot_general | solution.py:82
  120.2 144.6 %reduce-scatter.2.cloned.1.call-done = f32[128,64]{0,1:T(8,128)} async-done(((f32[4096,64]{0,1:T(8,128)}), f32[128,64]{0,1:T(8,128)}) %reduce-scatter.2.cloned.1.call-update) | async-done | bytes 32784 | tf_op jit(solution)/shard_map/reduce_scatter | solution.py:81
  264.8 0.9 multiply_reduce_fusion
  265.7 36.9 %psum.29 = f32[64]{0:T(128)S(1)} all-reduce(f32[64]{0:T(128)S(1)} %multiply_reduce_fusion), channel_id=1, replica_groups=mesh['param'=4,'ex'=8] {'param','ex'}, use_global_device_ids=true, to_apply=%region_3.4 | all-reduce | flops 64 | bytes 512 | tf_op jit(solution)/shard_map/psum | solution.py:92
  302.6 1.1 fusion.24
  303.6 41.8 %psum.30 = f32[64,64]{1,0:T(8,128)S(1)} all-reduce(f32[64,64]{1,0:T(8,128)S(1)} %fusion.24), channel_id=1, replica_groups=mesh['param'=4,'ex'=8] {'param','ex'}, use_global_device_ids=true, to_apply=%region_4.5 | all-reduce | flops 4096 | bytes 32768 | tf_op jit(solution)/shard_map/psum | solution.py:94
  345.6 5.8 %cholesky.15 = f32[64,64]{1,0:T(8,128)S(1)} custom-call(f32[64,64]{1,0:T(8,128)S(1)} %fusion.21), custom_call_target="Cholesky" | custom-call | tf_op jit(solution)/shard_map/jit(cholesky)/cholesky | solution.py:97
  352.1 0.7 fusion.14
  352.7 4.9 %custom-call.10 = f32[1,64,64]{1,2,0:T(8,128)S(1)} custom-call(f32[1,64,64]{2,1,0:T(8,128)S(1)} %fusion.14), custom_call_target="InvertDiagBlocksLowerTriangular" | custom-call | tf_op jit(solution)/shard_map/jit(_cho_solve)/triangular_solve | solution.py:103
  359.1 13.8 %psum.31 = f32[64,4]{0,1:T(4,128)S(1)} all-reduce(f32[64,4]{0,1:T(4,128)S(1)} %fusion.32), channel_id=1, replica_groups=mesh['param'=4,'ex'=8] {'ex'}, use_global_device_ids=true, to_apply=%region_7.8 | all-reduce | flops 256 | bytes 2048 | tf_op jit(solution)/shard_map/psum | solution.py:119
  (39 shorter events, 3.8 us)
Async XLA Ops:
  7.2 1.0 copy-start
  7.2 257.6 %reduce-scatter.2.cloned.1.call-start = ((), (), s32[]{:S(2)}) async-start(), calls=%async_computation.1 | async-start | bytes 1081344 | tf_op jit(solution)/shard_map/reduce_scatter | solution.py:81
  8.2 26.5 %copy-start.1 = (bf16[2,8,32,1024]{3,2,1,0:T(8,128)(2,1)S(1)}, bf16[2,8,32,1024]{3,2,1,0:T(8,128)(2,1)}, u32[]{:S(2)}) copy-start(bf16[2,8,32,1024]{3,2,1,0:T(8,128)(2,1)} %param.8) | copy-start | bytes 3145732
  43.2 10.0 %collective-permute-start = (bf16[1,8,8192]{2,0,1:T(2,128)(2,1)S(1)}, bf16[1,8,8192]{2,0,1:T(2,128)(2,1)S(1)}, u32[]{:S(2)}, u32[]{:S(2)}) collective-permute-start(bf16[1,8,8192]{2,0,1:T(2,128)(2,1)S(1)} %get-tuple-element.8), channel_id=1, source_target_pairs={{0,1},{1,2},{2,3},{3,4},{4,5},{5,6},{6,7},{7,0},{8,9},{9,10},{10,1... | collective-permute-start | bytes 393224 | tf_op jit(solution)/shard_map/ppermute | solution.py:78
  43.2 11.7 %collective-permute-start.1 = (bf16[1,8,8192]{2,0,1:T(2,128)(2,1)S(1)}, bf16[1,8,8192]{2,0,1:T(2,128)(2,1)S(1)}, u32[]{:S(2)}, u32[]{:S(2)}) collective-permute-start(bf16[1,8,8192]{2,0,1:T(2,128)(2,1)S(1)} %get-tuple-element.7), channel_id=1, source_target_pairs={{0,2},{1,3},{2,4},{3,5},{4,6},{5,7},{6,0},{7,1},{8,10},{9,11},{10,... | collective-permute-start | bytes 393224 | tf_op jit(solution)/shard_map/ppermute | solution.py:78
  44.8 31.2 %collective-permute-start.2 = (bf16[1,8,8192]{2,0,1:T(2,128)(2,1)}, bf16[1,8,8192]{2,0,1:T(2,128)(2,1)S(1)}, u32[]{:S(2)}, u32[]{:S(2)}) collective-permute-start(bf16[1,8,8192]{2,0,1:T(2,128)(2,1)} %get-tuple-element.6), channel_id=1, source_target_pairs={{0,3},{1,4},{2,5},{3,6},{4,7},{5,0},{6,1},{7,2},{8,11},{9,12},{10,... | collective-permute-start | bytes 393224 | tf_op jit(solution)/shard_map/ppermute | solution.py:78
  47.4 32.6 %collective-permute-start.3 = (bf16[1,8,8192]{2,0,1:T(2,128)(2,1)}, bf16[1,8,8192]{2,0,1:T(2,128)(2,1)S(1)}, u32[]{:S(2)}, u32[]{:S(2)}) collective-permute-start(bf16[1,8,8192]{2,0,1:T(2,128)(2,1)} %get-tuple-element.5), channel_id=1, source_target_pairs={{0,4},{1,5},{2,6},{3,7},{4,0},{5,1},{6,2},{7,3},{8,12},{9,13},{10,... | collective-permute-start | bytes 393224 | tf_op jit(solution)/shard_map/ppermute | solution.py:78
  48.6 35.3 %collective-permute-start.4 = (bf16[1,8,8192]{2,0,1:T(2,128)(2,1)}, bf16[1,8,8192]{2,0,1:T(2,128)(2,1)S(1)}, u32[]{:S(2)}, u32[]{:S(2)}) collective-permute-start(bf16[1,8,8192]{2,0,1:T(2,128)(2,1)} %get-tuple-element.4), channel_id=1, source_target_pairs={{0,5},{1,6},{2,7},{3,0},{4,1},{5,2},{6,3},{7,4},{8,13},{9,14},{10,... | collective-permute-start | bytes 393224 | tf_op jit(solution)/shard_map/ppermute | solution.py:78
  53.3 34.6 %collective-permute-start.5 = (bf16[1,8,8192]{2,0,1:T(2,128)(2,1)}, bf16[1,8,8192]{2,0,1:T(2,128)(2,1)S(1)}, u32[]{:S(2)}, u32[]{:S(2)}) collective-permute-start(bf16[1,8,8192]{2,0,1:T(2,128)(2,1)} %get-tuple-element.3), channel_id=1, source_target_pairs={{0,6},{1,7},{2,0},{3,1},{4,2},{5,3},{6,4},{7,5},{8,14},{9,15},{10,... | collective-permute-start | bytes 393224 | tf_op jit(solution)/shard_map/ppermute | solution.py:78
  54.9 36.9 %collective-permute-start.6 = (bf16[1,8,8192]{2,0,1:T(2,128)(2,1)}, bf16[1,8,8192]{2,0,1:T(2,128)(2,1)S(1)}, u32[]{:S(2)}, u32[]{:S(2)}) collective-permute-start(bf16[1,8,8192]{2,0,1:T(2,128)(2,1)} %get-tuple-element.2), channel_id=1, source_target_pairs={{0,7},{1,0},{2,1},{3,2},{4,3},{5,4},{6,5},{7,6},{8,15},{9,8},{10,9... | collective-permute-start | bytes 393224 | tf_op jit(solution)/shard_map/ppermute | solution.py:78
  95.8 24.4 %copy-start.2 = (s32[64]{0:T(128)S(1)}, s32[64]{0:T(128)}, u32[]{:S(2)}) copy-start(s32[64]{0:T(128)} %param.13) | copy-start | bytes 772
  120.1 238.8 %copy-start.3 = (s32[8]{0:T(128)S(1)}, s32[8]{0:T(128)}, u32[]{:S(2)}) copy-start(s32[8]{0:T(128)} %param.12) | copy-start | bytes 100
  358.9 14.7 %copy-start.4 = (f32[64,8]{0,1:T(8,128)}, f32[64,8]{0,1:T(8,128)S(1)}, u32[]{:S(2)}) copy-start(f32[64,8]{0,1:T(8,128)S(1)} %convolution_multiply_fusion) | copy-start | bytes 6148
Sparse Core Ops, SparseCore 0:
  120.3 144.4 reduce-scatter.1
